TPU v7x, 32 devices: a whole 2x2x4 slice. The times are simulated.
32 devices in a mesh: leaf: 8 (over z, y), row: 4 (over x, core).
Axes of the slice: x: 2, y: 2, z: 4, core: 2. Of those that a mesh axis runs over, the one named last changes fastest.
Arguments:
- panel0: float32 [12288, 512], P(('leaf', 'row')), may hold values from -3 to 30, as said below
- panel1: float32 [6144, 512], P(('leaf', 'row')), may hold values from -3 to 30
- panel2: float32 [3072, 512], P(('leaf', 'row')), may hold values from -3 to 30
- panel3: float32 [1536, 512], P(('leaf', 'row')), may hold values from -3 to 30
- maps1: int32 [8, 8], replicated, may hold values from 0 to 11, as said below
- maps2: int32 [4, 8], replicated, may hold values from 0 to 11, as said below
- maps3: int32 [2, 8], replicated, may hold values from 0 to 11, as said below
Outputs:
- update_top: float32 [1024, 1024], P(('leaf', 'row'))
Inputs may be any that keep to these rules, and one draw needn't show every extreme that they name: `panel0`: each front's first 512 rows form a symmetric matrix, and every assembled pivot block is positive definite. `maps1`: each row lists distinct parent block numbers. `maps2`: each row lists distinct parent block numbers. `maps3`: each row lists distinct parent block numbers.
All inputs are finite; a program needn't handle non-finite values.
Results may differ from a plain program's by a relative error of at most 0.0003.
Values sent between devices are 32-bit elements; how exact they have to be, the bound alone decides.
A program may use at most 128 MiB of HBM per device.

v0:
```python
import jax
import jax.numpy as jnp
from jax import lax
from jax.sharding import PartitionSpec as P

BLOCK = 128
PIV = 512
UPD = 1024
exact_mode = lax.Precision.HIGHEST


def partner(block, axis, stride):
    count = lax.axis_size(axis)
    route = []
    for low in range(count):
        high = low | 1 << stride
        if high != low and high < count:
            route += [(low, high), (high, low)]
    return lax.ppermute(block, axis, route)


def extend_add(update, blocks):
    parent_blocks = (PIV + UPD) // BLOCK
    child_blocks = blocks.shape[0]
    onehot = (blocks[:, None] == jnp.arange(parent_blocks, dtype=jnp.int32)[None, :]).astype(
        jnp.float32
    )
    tile_grid = update.reshape(child_blocks, BLOCK, child_blocks, BLOCK)
    spread = jnp.einsum("ia,ixjy->axjy", onehot, tile_grid, precision=exact_mode)
    placed = jnp.einsum("axjy,jb->axby", spread, onehot, precision=exact_mode)
    return placed.reshape(parent_blocks * BLOCK, parent_blocks * BLOCK)


def exact_dot(left, right):
    return jnp.dot(left, right, precision=exact_mode, preferred_element_type=jnp.float32)


def inverse_factor(pivot_block):
    tile_count = PIV // BLOCK
    identity = jnp.eye(BLOCK, dtype=jnp.float32)
    remaining = pivot_block
    lower_tiles = {}
    diag_inverse = []
    for column_tile in range(tile_count):
        offset = column_tile * BLOCK
        diag_factor = jnp.linalg.cholesky(
            remaining[offset : offset + BLOCK, offset : offset + BLOCK]
        )
        tile_inverse = jax.scipy.linalg.solve_triangular(diag_factor, identity, lower=True)
        diag_inverse.append(tile_inverse)
        if column_tile + 1 < tile_count:
            below_rows = exact_dot(
                remaining[offset + BLOCK :, offset : offset + BLOCK], tile_inverse.T
            )
            for row_tile in range(column_tile + 1, tile_count):
                start_row = (row_tile - column_tile - 1) * BLOCK
                lower_tiles[row_tile, column_tile] = below_rows[start_row : start_row + BLOCK]
            trailing_part = remaining[offset + BLOCK :, offset + BLOCK :] - exact_dot(
                below_rows, below_rows.T
            )
            remaining = remaining.at[offset + BLOCK :, offset + BLOCK :].set(trailing_part)
    inverse_tiles = {}
    for column_tile in range(tile_count):
        inverse_tiles[column_tile, column_tile] = diag_inverse[column_tile]
        for row_tile in range(column_tile + 1, tile_count):
            accumulated = jnp.zeros((BLOCK, BLOCK), jnp.float32)
            for middle in range(column_tile, row_tile):
                accumulated = accumulated + exact_dot(
                    lower_tiles[row_tile, middle], inverse_tiles[middle, column_tile]
                )
            inverse_tiles[row_tile, column_tile] = -exact_dot(diag_inverse[row_tile], accumulated)
    zero_tile = jnp.zeros((BLOCK, BLOCK), jnp.float32)
    tile_rows = []
    for row_tile in range(tile_count):
        pieces = [
            inverse_tiles[row_tile, column_tile] if column_tile <= row_tile else zero_tile
            for column_tile in range(tile_count)
        ]
        tile_rows.append(jnp.concatenate(pieces, axis=1))
    return jnp.concatenate(tile_rows, axis=0)


def group_total(partial_value, level_index):
    portion = lax.psum_scatter(partial_value, "row", scatter_dimension=1, tiled=True)
    for bit_number in range(level_index):
        portion = portion + partner(portion, "leaf", bit_number)
    assembled = lax.all_gather(portion, "row", axis=1, tiled=True)
    return assembled


def body(panel0, panel1, panel2, panel3, maps1, maps2, maps3):
    panels = (panel0, panel1, panel2, panel3)
    block_maps = (maps1, maps1, maps2, maps3)
    row_devices = lax.axis_size("row")
    leaf_index = lax.axis_index("leaf")
    row_index = lax.axis_index("row")
    schur = jnp.zeros((UPD, UPD), jnp.float32)
    for level_index in range(4):
        group_leaves = 2**level_index
        position = leaf_index % group_leaves * row_devices + row_index
        group_devices = group_leaves * row_devices
        panel_rows = panels[level_index]
        row_count = panel_rows.shape[0]
        if level_index == 0:
            partial_value = jnp.zeros((PIV + UPD, PIV), jnp.float32)
            trailing = jnp.zeros((UPD, UPD), jnp.float32)
        else:
            child_front = leaf_index // (group_leaves // 2)
            blocks = lax.dynamic_index_in_dim(
                block_maps[level_index], child_front, 0, keepdims=False
            )
            upper = extend_add(schur, blocks)
            partial_value = upper[:, :PIV]
            trailing = upper[PIV:, PIV:]
        start = position * row_count
        current = lax.dynamic_slice_in_dim(partial_value, start, row_count, 0)
        partial_value = lax.dynamic_update_slice_in_dim(
            partial_value, current + panel_rows, start, 0
        )
        assembled = group_total(partial_value, level_index)
        inverse = inverse_factor(assembled[:PIV])
        column_count = PIV // group_devices
        picked = lax.dynamic_slice_in_dim(inverse, position * column_count, column_count, 0)
        columns = exact_dot(assembled[PIV:], picked.T)
        schur = trailing - exact_dot(columns, columns.T)
    sub_rows = UPD // (8 * row_devices)
    grouped = jnp.swapaxes(schur.reshape(8, row_devices, sub_rows, UPD), 0, 1)
    shared = lax.psum_scatter(grouped, "row", scatter_dimension=0, tiled=True)
    current = shared[0]
    for bit_number in (2, 1, 0):
        half_count = current.shape[0] // 2
        upper_side = leaf_index // 2**bit_number % 2
        lower_half = current[:half_count]
        upper_half = current[half_count:]
        kept_half = jnp.where(upper_side == 1, upper_half, lower_half)
        given_half = jnp.where(upper_side == 1, lower_half, upper_half)
        current = kept_half + partner(given_half, "leaf", bit_number)
    return current.reshape(sub_rows, UPD)


def solution(mesh):
    placed = (
        P(("leaf", "row"), None),
        P(("leaf", "row"), None),
        P(("leaf", "row"), None),
        P(("leaf", "row"), None),
        P(),
        P(),
        P(),
    )
    return jax.shard_map(
        body, mesh=mesh, in_specs=placed, out_specs=P(("leaf", "row"), None), check_vma=False
    )
```

profile of v0, /device:TPU:0, one launch (start us, length us, event | category | flops | bytes accessed | tf_op | source)
XLA Modules:
  0.0 1117.7 jit_solution(9129842647226602034)
XLA Ops:
  12.2 40.7 %reduce-scatter.8.cloned.1.call-done = f32[1536,128]{0,1:T(8,128)} async-done(((f32[1536,512]{0,1:T(8,128)}), f32[1536,128]{0,1:T(8,128)}) %reduce-scatter.8.cloned.1.call-update) | async-done | bytes 786448 | tf_op jit(solution)/shard_map/reduce_scatter | solution.py:84
  54.0 29.0 %all-gather.5.cloned.1.call-done = f32[1536,512]{0,1:T(8,128)} async-done(((f32[1536,128]{0,1:T(8,128)}), f32[1536,512]{0,1:T(8,128)}) %all-gather.5.cloned.1.call-update) | async-done | bytes 3145744 | tf_op jit(solution)/shard_map/all_gather | solution.py:87
  111.2 11.7 %cholesky.265 = f32[128,128]{1,0:T(8,128)S(1)} custom-call(f32[128,128]{1,0:T(8,128)S(1)} %fusion.202), custom_call_target="Cholesky" | custom-call | tf_op jit(solution)/shard_map/jit(cholesky)/cholesky | solution.py:46
  135.7 11.7 %cholesky.276 = f32[128,128]{1,0:T(8,128)S(1)} custom-call(f32[128,128]{1,0:T(8,128)S(1)} %fusion.200), custom_call_target="Cholesky" | custom-call | tf_op jit(solution)/shard_map/jit(cholesky)/cholesky | solution.py:46
  161.2 11.8 %cholesky.287 = f32[128,128]{1,0:T(8,128)S(1)} custom-call(f32[128,128]{1,0:T(8,128)S(1)} %fusion.198), custom_call_target="Cholesky" | custom-call | tf_op jit(solution)/shard_map/jit(cholesky)/cholesky | solution.py:46
  232.9 38.4 %reduce-scatter.10.cloned.1.call-done = f32[1536,128]{0,1:T(8,128)} async-done(((f32[1536,512]{0,1:T(8,128)}), f32[1536,128]{0,1:T(8,128)}) %reduce-scatter.10.cloned.1.call-update) | async-done | bytes 786448 | tf_op jit(solution)/shard_map/reduce_scatter | solution.py:84
  272.8 17.8 %collective-permute-done = f32[1536,128]{0,1:T(8,128)S(1)} collective-permute-done((f32[1536,128]{0,1:T(8,128)}, f32[1536,128]{0,1:T(8,128)S(1)}, u32[]{:S(2)}, u32[]{:S(2)}) %collective-permute-start) | collective-permute-done | bytes 786464 | tf_op jit(solution)/shard_map/ppermute | solution.py:19
  294.6 26.9 %all-gather.7.cloned.1.call-done = f32[1536,512]{0,1:T(8,128)} async-done(((f32[1536,128]{0,1:T(8,128)}), f32[1536,512]{0,1:T(8,128)}) %all-gather.7.cloned.1.call-update) | async-done | bytes 3145744 | tf_op jit(solution)/shard_map/all_gather | solution.py:87
  349.8 11.7 %cholesky.309 = f32[128,128]{1,0:T(8,128)S(1)} custom-call(f32[128,128]{1,0:T(8,128)S(1)} %fusion.194), custom_call_target="Cholesky" | custom-call | tf_op jit(solution)/shard_map/jit(cholesky)/cholesky | solution.py:46
  374.0 11.7 %cholesky.320 = f32[128,128]{1,0:T(8,128)S(1)} custom-call(f32[128,128]{1,0:T(8,128)S(1)} %fusion.192), custom_call_target="Cholesky" | custom-call | tf_op jit(solution)/shard_map/jit(cholesky)/cholesky | solution.py:46
  399.4 12.1 %cholesky.331 = f32[128,128]{1,0:T(8,128)S(1)} custom-call(f32[128,128]{1,0:T(8,128)S(1)} %fusion.190), custom_call_target="Cholesky" | custom-call | tf_op jit(solution)/shard_map/jit(cholesky)/cholesky | solution.py:46
  469.9 38.4 %reduce-scatter.12.cloned.1.call-done = f32[1536,128]{0,1:T(8,128)} async-done(((f32[1536,512]{0,1:T(8,128)}), f32[1536,128]{0,1:T(8,128)}) %reduce-scatter.12.cloned.1.call-update) | async-done | bytes 786448 | tf_op jit(solution)/shard_map/reduce_scatter | solution.py:84
  509.7 17.9 %collective-permute-done.1 = f32[1536,128]{0,1:T(8,128)S(1)} collective-permute-done((f32[1536,128]{0,1:T(8,128)}, f32[1536,128]{0,1:T(8,128)S(1)}, u32[]{:S(2)}, u32[]{:S(2)}) %collective-permute-start.1) | collective-permute-done | bytes 786464 | tf_op jit(solution)/shard_map/ppermute | solution.py:19
  530.4 16.8 %collective-permute-done.2 = f32[1536,128]{0,1:T(8,128)S(1)} collective-permute-done((f32[1536,128]{0,1:T(8,128)S(1)}, f32[1536,128]{0,1:T(8,128)S(1)}, u32[]{:S(2)}, u32[]{:S(2)}) %collective-permute-start.2) | collective-permute-done | bytes 786464 | tf_op jit(solution)/shard_map/ppermute | solution.py:19
  549.6 27.3 %all-gather.9.cloned.1.call-done = f32[1536,512]{0,1:T(8,128)} async-done(((f32[1536,128]{0,1:T(8,128)}), f32[1536,512]{0,1:T(8,128)}) %all-gather.9.cloned.1.call-update) | async-done | bytes 3145744 | tf_op jit(solution)/shard_map/all_gather | solution.py:87
  654.8 11.9 %cholesky.375 = f32[128,128]{1,0:T(8,128)S(1)} custom-call(f32[128,128]{1,0:T(8,128)S(1)} %fusion.182), custom_call_target="Cholesky" | custom-call | tf_op jit(solution)/shard_map/jit(cholesky)/cholesky | solution.py:46
  725.1 38.4 %reduce-scatter.14.cloned.1.call-done = f32[1536,128]{0,1:T(8,128)} async-done(((f32[1536,512]{0,1:T(8,128)}), f32[1536,128]{0,1:T(8,128)}) %reduce-scatter.14.cloned.1.call-update) | async-done | bytes 786448 | tf_op jit(solution)/shard_map/reduce_scatter | solution.py:84
  764.9 17.8 %collective-permute-done.3 = f32[1536,128]{0,1:T(8,128)S(1)} collective-permute-done((f32[1536,128]{0,1:T(8,128)}, f32[1536,128]{0,1:T(8,128)S(1)}, u32[]{:S(2)}, u32[]{:S(2)}) %collective-permute-start.3) | collective-permute-done | bytes 786464 | tf_op jit(solution)/shard_map/ppermute | solution.py:19
  785.6 16.7 %collective-permute-done.4 = f32[1536,128]{0,1:T(8,128)S(1)} collective-permute-done((f32[1536,128]{0,1:T(8,128)S(1)}, f32[1536,128]{0,1:T(8,128)S(1)}, u32[]{:S(2)}, u32[]{:S(2)}) %collective-permute-start.4) | collective-permute-done | bytes 786464 | tf_op jit(solution)/shard_map/ppermute | solution.py:19
  804.9 32.7 %collective-permute-done.5 = f32[1536,128]{0,1:T(8,128)S(1)} collective-permute-done((f32[1536,128]{0,1:T(8,128)S(1)}, f32[1536,128]{0,1:T(8,128)S(1)}, u32[]{:S(2)}, u32[]{:S(2)}) %collective-permute-start.5) | collective-permute-done | bytes 786464 | tf_op jit(solution)/shard_map/ppermute | solution.py:19
  838.9 28.4 %all-gather.11.cloned.1.call-done = f32[1536,512]{0,1:T(8,128)} async-done(((f32[1536,128]{0,1:T(8,128)}), f32[1536,512]{0,1:T(8,128)}) %all-gather.11.cloned.1.call-update) | async-done | bytes 3145744 | tf_op jit(solution)/shard_map/all_gather | solution.py:87
  945.8 11.9 %cholesky.419 = f32[128,128]{1,0:T(8,128)S(1)} custom-call(f32[128,128]{1,0:T(8,128)S(1)} %fusion.174), custom_call_target="Cholesky" | custom-call | tf_op jit(solution)/shard_map/jit(cholesky)/cholesky | solution.py:46
  982.2 84.4 %all-reduce.7.cloned.1.call-done = f32[4,8,32,1024]{3,2,0,1:T(8,128)} async-done(((f32[4,8,32,1024]{3,2,0,1:T(8,128)}), f32[4,8,32,1024]{3,2,0,1:T(8,128)}) %all-reduce.7.cloned.1.call-update) | async-done | bytes 4194320
  1072.9 23.1 %collective-permute-done.6 = f32[4,32,1024]{2,1,0:T(8,128)S(1)} collective-permute-done((f32[4,32,1024]{2,1,0:T(8,128)S(1)}, f32[4,32,1024]{2,1,0:T(8,128)S(1)}, u32[]{:S(2)}, u32[]{:S(2)}) %collective-permute-start.6) | collective-permute-done | bytes 524320 | tf_op jit(solution)/shard_map/ppermute | solution.py:19
  (340 shorter events, 513.2 us)
Async XLA Ops:
  6.5 47.5 %copy-start = (s32[8,8]{1,0:T(8,128)S(1)}, s32[8,8]{1,0:T(8,128)}, u32[]{:S(2)}) copy-start(s32[8,8]{1,0:T(8,128)} %param.38) | copy-start | bytes 772
  6.5 46.4 %reduce-scatter.8.cloned.1.call-start = ((), (), s32[]{:S(2)}) async-start(), calls=%async_computation.4 | async-start | bytes 3932160 | tf_op jit(solution)/shard_map/reduce_scatter | solution.py:84
  8.8 44.2 %copy-start.6 = (f32[192,512]{1,0:T(8,128)S(1)}, f32[192,512]{1,0:T(8,128)}, u32[]{:S(2)}) copy-start(f32[192,512]{1,0:T(8,128)} %param.35) | copy-start | bytes 1179652
  12.1 70.9 %all-gather.5.cloned.1.call-start = ((), (), s32[]{:S(2)}) async-start(), calls=%async_computation.5 | async-start | bytes 3932160 | tf_op jit(solution)/shard_map/all_gather | solution.py:87
  52.9 218.4 %reduce-scatter.10.cloned.1.call-start = ((), (), s32[]{:S(2)}) async-start(), calls=%async_computation.6 | async-start | bytes 3932160 | tf_op jit(solution)/shard_map/reduce_scatter | solution.py:84
  224.4 68.7 %copy-start.7 = (f32[96,512]{1,0:T(8,128)S(1)}, f32[96,512]{1,0:T(8,128)}, u32[]{:S(2)}) copy-start(f32[96,512]{1,0:T(8,128)} %param.36) | copy-start | bytes 589828
  232.9 88.6 %all-gather.7.cloned.1.call-start = ((), (), s32[]{:S(2)}) async-start(), calls=%async_computation.7 | async-start | bytes 3932160 | tf_op jit(solution)/shard_map/all_gather | solution.py:87
  271.3 19.3 %collective-permute-start = (f32[1536,128]{0,1:T(8,128)}, f32[1536,128]{0,1:T(8,128)S(1)}, u32[]{:S(2)}, u32[]{:S(2)}) collective-permute-start(f32[1536,128]{0,1:T(8,128)} %reduce-scatter.10.cloned.1.call-done), channel_id=1, source_target_pairs={{0,4},{4,0},{8,12},{12,8},{16,20},{20,16},{24,28},{28,24},{1,5},{5... | collective-permute-start | bytes 2359304 | tf_op jit(solution)/shard_map/ppermute | solution.py:19
  292.8 215.4 %reduce-scatter.12.cloned.1.call-start = ((), (), s32[]{:S(2)}) async-start(), calls=%async_computation.8 | async-start | bytes 3932160 | tf_op jit(solution)/shard_map/reduce_scatter | solution.py:84
  468.2 80.6 %copy-start.8 = (f32[48,512]{1,0:T(8,128)S(1)}, f32[48,512]{1,0:T(8,128)}, u32[]{:S(2)}) copy-start(f32[48,512]{1,0:T(8,128)} %param.37) | copy-start | bytes 294916
  468.2 81.4 %copy-start.9 = (s32[2,8]{1,0:T(2,128)S(1)}, s32[2,8]{1,0:T(2,128)}, u32[]{:S(2)}) copy-start(s32[2,8]{1,0:T(2,128)} %param.40) | copy-start | bytes 196
  469.8 107.1 %all-gather.9.cloned.1.call-start = ((), (), s32[]{:S(2)}) async-start(), calls=%async_computation.9 | async-start | bytes 3932160 | tf_op jit(solution)/shard_map/all_gather | solution.py:87
  508.3 19.3 %collective-permute-start.1 = (f32[1536,128]{0,1:T(8,128)}, f32[1536,128]{0,1:T(8,128)S(1)}, u32[]{:S(2)}, u32[]{:S(2)}) collective-permute-start(f32[1536,128]{0,1:T(8,128)} %reduce-scatter.12.cloned.1.call-done), channel_id=1, source_target_pairs={{0,4},{4,0},{8,12},{12,8},{16,20},{20,16},{24,28},{28,24},{1,5},{5... | collective-permute-start | bytes 2359304 | tf_op jit(solution)/shard_map/ppermute | solution.py:19
  528.9 18.3 %collective-permute-start.2 = (f32[1536,128]{0,1:T(8,128)S(1)}, f32[1536,128]{0,1:T(8,128)S(1)}, u32[]{:S(2)}, u32[]{:S(2)}) collective-permute-start(f32[1536,128]{0,1:T(8,128)S(1)} %add.230), channel_id=1, source_target_pairs={{0,8},{8,0},{4,12},{12,4},{16,24},{24,16},{20,28},{28,20},{1,9},{9... | collective-permute-start | bytes 2359304 | tf_op jit(solution)/shard_map/ppermute | solution.py:19
  548.2 215.2 %reduce-scatter.14.cloned.1.call-start = ((), (), s32[]{:S(2)}) async-start(), calls=%async_computation.10 | async-start | bytes 3932160 | tf_op jit(solution)/shard_map/reduce_scatter | solution.py:84
  725.0 142.4 %all-gather.11.cloned.1.call-start = ((), (), s32[]{:S(2)}) async-start(), calls=%async_computation.11 | async-start | bytes 3932160 | tf_op jit(solution)/shard_map/all_gather | solution.py:87
  763.4 19.3 %collective-permute-start.3 = (f32[1536,128]{0,1:T(8,128)}, f32[1536,128]{0,1:T(8,128)S(1)}, u32[]{:S(2)}, u32[]{:S(2)}) collective-permute-start(f32[1536,128]{0,1:T(8,128)} %reduce-scatter.14.cloned.1.call-done), channel_id=1, source_target_pairs={{0,4},{4,0},{8,12},{12,8},{16,20},{20,16},{24,28},{28,24},{1,5},{5... | collective-permute-start | bytes 2359304 | tf_op jit(solution)/shard_map/ppermute | solution.py:19
  784.0 18.3 %collective-permute-start.4 = (f32[1536,128]{0,1:T(8,128)S(1)}, f32[1536,128]{0,1:T(8,128)S(1)}, u32[]{:S(2)}, u32[]{:S(2)}) collective-permute-start(f32[1536,128]{0,1:T(8,128)S(1)} %add.241), channel_id=1, source_target_pairs={{0,8},{8,0},{4,12},{12,4},{16,24},{24,16},{20,28},{28,20},{1,9},{9... | collective-permute-start | bytes 2359304 | tf_op jit(solution)/shard_map/ppermute | solution.py:19
  802.4 35.2 %collective-permute-start.5 = (f32[1536,128]{0,1:T(8,128)S(1)}, f32[1536,128]{0,1:T(8,128)S(1)}, u32[]{:S(2)}, u32[]{:S(2)}) collective-permute-start(f32[1536,128]{0,1:T(8,128)S(1)} %add.242), channel_id=1, source_target_pairs={{0,16},{16,0},{4,20},{20,4},{8,24},{24,8},{12,28},{28,12},{1,17},{... | collective-permute-start | bytes 2359304 | tf_op jit(solution)/shard_map/ppermute | solution.py:19
  838.7 228.0 %all-reduce.7.cloned.1.call-start = ((), (), s32[]{:S(2)}) async-start(), calls=%async_computation.12 | async-start | bytes 8388608
  1066.6 44.3 %copy-start.1 = (s32[8,8]{1,0:T(8,128)S(1)}, s32[8,8]{1,0:T(8,128)}, u32[]{:S(2)}) copy-start(s32[8,8]{1,0:T(8,128)} %param.38) | copy-start | bytes 772
  1070.4 25.5 %collective-permute-start.6 = (f32[4,32,1024]{2,1,0:T(8,128)S(1)}, f32[4,32,1024]{2,1,0:T(8,128)S(1)}, u32[]{:S(2)}, u32[]{:S(2)}) collective-permute-start(f32[4,32,1024]{2,1,0:T(8,128)S(1)} %fusion.22), channel_id=1, source_target_pairs={{0,16},{16,0},{4,20},{20,4},{8,24},{24,8},{12,28},{28,12},{1,17},{... | collective-permute-start | bytes 1572872 | tf_op jit(solution)/shard_map/ppermute | solution.py:19
  1097.8 7.4 collective-permute-start.7
  1105.3 5.0 collective-permute-start.8
  (5 other events, 7.2 us)
Sparse Core Ops, SparseCore 0:
  12.3 40.5 reduce-scatter.7
  54.5 28.5 all-gather.4
  233.0 38.2 reduce-scatter.9
  293.0 28.5 all-gather.6
  469.9 38.2 reduce-scatter.11
  548.4 28.4 all-gather.8
  725.1 38.2 reduce-scatter.13
  838.8 28.5 all-gather.10
  981.1 85.4 all-reduce.6
where the time goes:
time: 1130 us; the launch traced here: 1120 us
  waiting for transfers between devices  505 us (45%)
  other arithmetic  388 us (34%)
  matrix products  115 us (10%)
  local copies, waits for them, and re-layouts  78.7 us (7%)
  starting transfers between devices  15.7 us (1%)
  between operations  15.2 us (1%)
    another operation x48, other arithmetic, inverse_factor(): jnp.linalg.cholesky(remaining[offset:offset + BLOCK, offset:offset + BLOCK])  199 us
    another operation x32, other arithmetic, inverse_factor(): jax.scipy.linalg.solve_triangular(diag_factor, identity, lower=True)  169 us
    reduce_scatter x4, waiting for transfers between devices, group_total(): lax.psum_scatter(partial_value, 'row', scatter_dimension=1, tiled=True)  156 us
    ppermute x9, waiting for transfers between devices, partner(): return lax.ppermute(block, axis, route)  153 us
    all_gather x4, waiting for transfers between devices, group_total(): assembled = lax.all_gather(portion, 'row', axis=1, tiled=True)  112 us
    unnamed x10, waiting for transfers between devices  84.6 us
    dot_general x96, matrix products, exact_dot(): jnp.dot(left, right, precision=exact_mode, preferred_element_type=jnp.flo...  72.2 us
    unnamed x36, local copies, waits for them, and re-layouts  47.8 us
  transfers between devices with their start and end apart: 18, of which 18 were waited for; matrix products, arithmetic and copies ran while one was open for 0% of the time, Pallas kernels for 0%

commit v1 on v0

--- a/solution.py
+++ b/solution.py
@@ -84,7 +84,14 @@
     portion = lax.psum_scatter(partial_value, "row", scatter_dimension=1, tiled=True)
     for bit_number in range(level_index):
         portion = portion + partner(portion, "leaf", bit_number)
-    assembled = lax.all_gather(portion, "row", axis=1, tiled=True)
+    ways = lax.axis_size("row")
+    parts = [portion]
+    for far in range(1, ways):
+        parts.append(
+            lax.ppermute(parts[far - 1], "row", [(d, (d - 1) % ways) for d in range(ways)])
+        )
+    line = jnp.concatenate(parts, axis=1)
+    assembled = jnp.roll(line, lax.axis_index("row") * portion.shape[1], axis=1)
     return assembled
 
 

time: 1130 us -> 1320 us (1.17)
  matrix products: 115 us -> 182 us
  other arithmetic: 388 us -> 450 us
  local copies, waits for them, and re-layouts: 78.7 us -> 117 us
  starting transfers between devices: 15.7 us -> 29.9 us
    all_gather x4 -> x0, waiting for transfers between devices: 112 us -> none  [group_total(): assembled = lax.all_gather(portion, 'row', axis=1, tiled=True)]
    ppermute x0 -> x12, waiting for transfers between devices: none -> 111 us  [group_total(): lax.ppermute(parts[far - 1], 'row', [(d, (d - 1) % ways) for d in range(w...]
    dot_general x96, matrix products: 72.2 us -> 132 us  [exact_dot(): jnp.dot(left, right, precision=exact_mode, preferred_element_type=jnp.flo...]
    another operation x32, other arithmetic: 169 us -> 189 us  [inverse_factor(): jax.scipy.linalg.solve_triangular(diag_factor, identity, lower=True)]
    concatenate x0 -> x4, other arithmetic: none -> 18 us  [group_total(): assembled = jnp.roll(line, lax.axis_index('row') * portion.shape[1], axis=1)]
    another operation x48, other arithmetic: 199 us -> 216 us  [inverse_factor(): jnp.linalg.cholesky(remaining[offset:offset + BLOCK, offset:offset + BLOCK])]
    ppermute x0 -> x12, starting transfers between devices: none -> 15.2 us  [group_total(): lax.ppermute(parts[far - 1], 'row', [(d, (d - 1) % ways) for d in range(w...]
    unnamed x36 -> x106, local copies, waits for them, and re-layouts: 47.8 us -> 63 us
  transfers between devices with their start and end apart: 18 -> 26, of which waited for: 18 -> 26; matrix products, arithmetic and copies ran while one was open for 0% -> 0% of each run, Pallas kernels for 0% -> 0%
where the time goes in v1:
time: 1320 us; the launch traced here: 1310 us
  waiting for transfers between devices  513 us (39%)
  other arithmetic  450 us (34%)
  matrix products  182 us (14%)
  local copies, waits for them, and re-layouts  117 us (9%)
  starting transfers between devices  29.9 us (2%)
  between operations  14.9 us (1%)
    another operation x48, other arithmetic, inverse_factor(): jnp.linalg.cholesky(remaining[offset:offset + BLOCK, offset:offset + BLOCK])  216 us
    another operation x32, other arithmetic, inverse_factor(): jax.scipy.linalg.solve_triangular(diag_factor, identity, lower=True)  189 us
    reduce_scatter x4, waiting for transfers between devices, group_total(): lax.psum_scatter(partial_value, 'row', scatter_dimension=1, tiled=True)  162 us
    ppermute x9, waiting for transfers between devices, partner(): return lax.ppermute(block, axis, route)  153 us
    dot_general x96, matrix products, exact_dot(): jnp.dot(left, right, precision=exact_mode, preferred_element_type=jnp.flo...  132 us
    ppermute x12, waiting for transfers between devices, group_total(): lax.ppermute(parts[far - 1], 'row', [(d, (d - 1) % ways) for d in range(w...  111 us
    unnamed x6, waiting for transfers between devices  86.9 us
    unnamed x106, local copies, waits for them, and re-layouts  63 us
  transfers between devices with their start and end apart: 26, of which 26 were waited for; matrix products, arithmetic and copies ran while one was open for 0% of the time, Pallas kernels for 0%

profile of v1, /device:TPU:0, one launch (start us, length us, event | category | flops | bytes accessed | tf_op | source)
XLA Modules:
  0.0 1306.5 jit_solution(7443900182954735374)
XLA Ops:
  11.8 40.7 %reduce-scatter.8.cloned.1.call-done = f32[1536,128]{0,1:T(8,128)} async-done(((f32[1536,512]{0,1:T(8,128)}), f32[1536,128]{0,1:T(8,128)}) %reduce-scatter.8.cloned.1.call-update) | async-done | bytes 786448 | tf_op jit(solution)/shard_map/reduce_scatter | solution.py:84
  90.6 11.7 cholesky.254
  148.0 13.2 %cholesky.276 = f32[128,128]{1,0:T(8,128)} custom-call(f32[128,128]{1,0:T(8,128)} %fusion.228), custom_call_target="Cholesky" | custom-call | tf_op jit(solution)/shard_map/jit(cholesky)/cholesky | solution.py:46
  191.9 11.9 cholesky.287
  269.6 40.7 %reduce-scatter.10.cloned.1.call-done = f32[1536,128]{0,1:T(8,128)} async-done(((f32[1536,512]{0,1:T(8,128)}), f32[1536,128]{0,1:T(8,128)}) %reduce-scatter.10.cloned.1.call-update) | async-done | bytes 786448 | tf_op jit(solution)/shard_map/reduce_scatter | solution.py:84
  311.8 17.9 %collective-permute-done.3 = f32[1536,128]{0,1:T(8,128)S(1)} collective-permute-done((f32[1536,128]{0,1:T(8,128)}, f32[1536,128]{0,1:T(8,128)S(1)}, u32[]{:S(2)}, u32[]{:S(2)}) %collective-permute-start.3) | collective-permute-done | bytes 786464 | tf_op jit(solution)/shard_map/ppermute | solution.py:19
  369.6 11.7 cholesky.298
  426.8 13.2 %cholesky.320 = f32[128,128]{1,0:T(8,128)} custom-call(f32[128,128]{1,0:T(8,128)} %fusion.220), custom_call_target="Cholesky" | custom-call | tf_op jit(solution)/shard_map/jit(cholesky)/cholesky | solution.py:46
  472.0 13.5 %cholesky.331 = f32[128,128]{1,0:T(8,128)} custom-call(f32[128,128]{1,0:T(8,128)} %fusion.218), custom_call_target="Cholesky" | custom-call | tf_op jit(solution)/shard_map/jit(cholesky)/cholesky | solution.py:46
  556.4 40.2 %reduce-scatter.12.cloned.1.call-done = f32[1536,128]{0,1:T(8,128)} async-done(((f32[1536,512]{0,1:T(8,128)}), f32[1536,128]{0,1:T(8,128)}) %reduce-scatter.12.cloned.1.call-update) | async-done | bytes 786448 | tf_op jit(solution)/shard_map/reduce_scatter | solution.py:84
  598.1 17.8 %collective-permute-done.7 = f32[1536,128]{0,1:T(8,128)S(1)} collective-permute-done((f32[1536,128]{0,1:T(8,128)}, f32[1536,128]{0,1:T(8,128)S(1)}, u32[]{:S(2)}, u32[]{:S(2)}) %collective-permute-start.7) | collective-permute-done | bytes 786464 | tf_op jit(solution)/shard_map/ppermute | solution.py:19
  618.7 16.8 %collective-permute-done.8 = f32[1536,128]{0,1:T(8,128)S(1)} collective-permute-done((f32[1536,128]{0,1:T(8,128)S(1)}, f32[1536,128]{0,1:T(8,128)S(1)}, u32[]{:S(2)}, u32[]{:S(2)}) %collective-permute-start.8) | collective-permute-done | bytes 786464 | tf_op jit(solution)/shard_map/ppermute | solution.py:19
  674.5 11.7 cholesky.342
  731.7 13.2 %cholesky.364 = f32[128,128]{1,0:T(8,128)} custom-call(f32[128,128]{1,0:T(8,128)} %fusion.212), custom_call_target="Cholesky" | custom-call | tf_op jit(solution)/shard_map/jit(cholesky)/cholesky | solution.py:46
  776.9 13.4 %cholesky.375 = f32[128,128]{1,0:T(8,128)} custom-call(f32[128,128]{1,0:T(8,128)} %fusion.210), custom_call_target="Cholesky" | custom-call | tf_op jit(solution)/shard_map/jit(cholesky)/cholesky | solution.py:46
  861.1 40.1 %reduce-scatter.14.cloned.1.call-done = f32[1536,128]{0,1:T(8,128)} async-done(((f32[1536,512]{0,1:T(8,128)}), f32[1536,128]{0,1:T(8,128)}) %reduce-scatter.14.cloned.1.call-update) | async-done | bytes 786448 | tf_op jit(solution)/shard_map/reduce_scatter | solution.py:84
  902.8 17.8 %collective-permute-done.12 = f32[1536,128]{0,1:T(8,128)S(1)} collective-permute-done((f32[1536,128]{0,1:T(8,128)}, f32[1536,128]{0,1:T(8,128)S(1)}, u32[]{:S(2)}, u32[]{:S(2)}) %collective-permute-start.12) | collective-permute-done | bytes 786464 | tf_op jit(solution)/shard_map/ppermute | solution.py:19
  923.4 16.8 %collective-permute-done.13 = f32[1536,128]{0,1:T(8,128)S(1)} collective-permute-done((f32[1536,128]{0,1:T(8,128)S(1)}, f32[1536,128]{0,1:T(8,128)S(1)}, u32[]{:S(2)}, u32[]{:S(2)}) %collective-permute-start.13) | collective-permute-done | bytes 786464 | tf_op jit(solution)/shard_map/ppermute | solution.py:19
  942.7 32.7 %collective-permute-done.14 = f32[1536,128]{0,1:T(8,128)S(1)} collective-permute-done((f32[1536,128]{0,1:T(8,128)S(1)}, f32[1536,128]{0,1:T(8,128)S(1)}, u32[]{:S(2)}, u32[]{:S(2)}) %collective-permute-start.14) | collective-permute-done | bytes 786464 | tf_op jit(solution)/shard_map/ppermute | solution.py:19
  1014.3 11.7 cholesky.386
  1077.8 13.2 %cholesky.408 = f32[128,128]{1,0:T(8,128)} custom-call(f32[128,128]{1,0:T(8,128)} %fusion.204), custom_call_target="Cholesky" | custom-call | tf_op jit(solution)/shard_map/jit(cholesky)/cholesky | solution.py:46
  1117.9 13.3 %cholesky.419 = f32[128,128]{1,0:T(8,128)} custom-call(f32[128,128]{1,0:T(8,128)} %fusion.202), custom_call_target="Cholesky" | custom-call | tf_op jit(solution)/shard_map/jit(cholesky)/cholesky | solution.py:46
  1168.6 86.8 %all-reduce.7.cloned.1.call-done = f32[4,8,32,1024]{3,2,0,1:T(8,128)} async-done(((f32[4,8,32,1024]{3,2,0,1:T(8,128)}), f32[4,8,32,1024]{3,2,0,1:T(8,128)}) %all-reduce.7.cloned.1.call-update) | async-done | bytes 4194320
  1261.7 23.1 %collective-permute-done.18 = f32[4,32,1024]{2,1,0:T(8,128)S(1)} collective-permute-done((f32[4,32,1024]{2,1,0:T(8,128)S(1)}, f32[4,32,1024]{2,1,0:T(8,128)S(1)}, u32[]{:S(2)}, u32[]{:S(2)}) %collective-permute-start.18) | collective-permute-done | bytes 524320 | tf_op jit(solution)/shard_map/ppermute | solution.py:19
  (426 shorter events, 748.6 us)
Async XLA Ops:
  6.5 46.0 %reduce-scatter.8.cloned.1.call-start = ((), (), s32[]{:S(2)}) async-start(), calls=%async_computation.4 | async-start | bytes 3932160 | tf_op jit(solution)/shard_map/reduce_scatter | solution.py:84
  11.8 298.5 %reduce-scatter.10.cloned.1.call-start = ((), (), s32[]{:S(2)}) async-start(), calls=%async_computation.5 | async-start | bytes 3932160 | tf_op jit(solution)/shard_map/reduce_scatter | solution.py:84
  52.5 9.8 collective-permute-start
  63.2 11.3 collective-permute-start.1
  74.5 11.4 collective-permute-start.2
  269.6 327.0 %reduce-scatter.12.cloned.1.call-start = ((), (), s32[]{:S(2)}) async-start(), calls=%async_computation.6 | async-start | bytes 3932160 | tf_op jit(solution)/shard_map/reduce_scatter | solution.py:84
  310.3 19.4 %collective-permute-start.3 = (f32[1536,128]{0,1:T(8,128)}, f32[1536,128]{0,1:T(8,128)S(1)}, u32[]{:S(2)}, u32[]{:S(2)}) collective-permute-start(f32[1536,128]{0,1:T(8,128)} %reduce-scatter.10.cloned.1.call-done), channel_id=1, source_target_pairs={{0,4},{4,0},{8,12},{12,8},{16,20},{20,16},{24,28},{28,24},{1,5},{5... | collective-permute-start | bytes 2359304 | tf_op jit(solution)/shard_map/ppermute | solution.py:19
  331.8 9.5 collective-permute-start.4
  342.2 11.4 collective-permute-start.5
  353.6 11.4 collective-permute-start.6
  556.4 344.9 %reduce-scatter.14.cloned.1.call-start = ((), (), s32[]{:S(2)}) async-start(), calls=%async_computation.7 | async-start | bytes 3932160 | tf_op jit(solution)/shard_map/reduce_scatter | solution.py:84
  596.6 19.3 %collective-permute-start.7 = (f32[1536,128]{0,1:T(8,128)}, f32[1536,128]{0,1:T(8,128)S(1)}, u32[]{:S(2)}, u32[]{:S(2)}) collective-permute-start(f32[1536,128]{0,1:T(8,128)} %reduce-scatter.12.cloned.1.call-done), channel_id=1, source_target_pairs={{0,4},{4,0},{8,12},{12,8},{16,20},{20,16},{24,28},{28,24},{1,5},{5... | collective-permute-start | bytes 2359304 | tf_op jit(solution)/shard_map/ppermute | solution.py:19
  617.2 18.3 %collective-permute-start.8 = (f32[1536,128]{0,1:T(8,128)S(1)}, f32[1536,128]{0,1:T(8,128)S(1)}, u32[]{:S(2)}, u32[]{:S(2)}) collective-permute-start(f32[1536,128]{0,1:T(8,128)S(1)} %add.238), channel_id=1, source_target_pairs={{0,8},{8,0},{4,12},{12,4},{16,24},{24,16},{20,28},{28,20},{1,9},{9... | collective-permute-start | bytes 2359304 | tf_op jit(solution)/shard_map/ppermute | solution.py:19
  636.5 9.5 collective-permute-start.9
  646.9 11.4 collective-permute-start.10
  658.3 11.4 collective-permute-start.11
  861.1 394.3 %all-reduce.7.cloned.1.call-start = ((), (), s32[]{:S(2)}) async-start(), calls=%async_computation.8 | async-start | bytes 8388608
  901.3 19.3 %collective-permute-start.12 = (f32[1536,128]{0,1:T(8,128)}, f32[1536,128]{0,1:T(8,128)S(1)}, u32[]{:S(2)}, u32[]{:S(2)}) collective-permute-start(f32[1536,128]{0,1:T(8,128)} %reduce-scatter.14.cloned.1.call-done), channel_id=1, source_target_pairs={{0,4},{4,0},{8,12},{12,8},{16,20},{20,16},{24,28},{28,24},{1,5},{5... | collective-permute-start | bytes 2359304 | tf_op jit(solution)/shard_map/ppermute | solution.py:19
  921.9 18.3 %collective-permute-start.13 = (f32[1536,128]{0,1:T(8,128)S(1)}, f32[1536,128]{0,1:T(8,128)S(1)}, u32[]{:S(2)}, u32[]{:S(2)}) collective-permute-start(f32[1536,128]{0,1:T(8,128)S(1)} %add.249), channel_id=1, source_target_pairs={{0,8},{8,0},{4,12},{12,4},{16,24},{24,16},{20,28},{28,20},{1,9},{9... | collective-permute-start | bytes 2359304 | tf_op jit(solution)/shard_map/ppermute | solution.py:19
  940.3 35.2 %collective-permute-start.14 = (f32[1536,128]{0,1:T(8,128)S(1)}, f32[1536,128]{0,1:T(8,128)S(1)}, u32[]{:S(2)}, u32[]{:S(2)}) collective-permute-start(f32[1536,128]{0,1:T(8,128)S(1)} %add.250), channel_id=1, source_target_pairs={{0,16},{16,0},{4,20},{20,4},{8,24},{24,8},{12,28},{28,12},{1,17},{... | collective-permute-start | bytes 2359304 | tf_op jit(solution)/shard_map/ppermute | solution.py:19
  976.5 9.5 collective-permute-start.15
  986.9 11.4 collective-permute-start.16
  998.3 11.4 collective-permute-start.17
  1259.2 25.5 %collective-permute-start.18 = (f32[4,32,1024]{2,1,0:T(8,128)S(1)}, f32[4,32,1024]{2,1,0:T(8,128)S(1)}, u32[]{:S(2)}, u32[]{:S(2)}) collective-permute-start(f32[4,32,1024]{2,1,0:T(8,128)S(1)} %fusion.50), channel_id=1, source_target_pairs={{0,16},{16,0},{4,20},{20,4},{8,24},{24,8},{12,28},{28,12},{1,17},{... | collective-permute-start | bytes 1572872 | tf_op jit(solution)/shard_map/ppermute | solution.py:19
  (48 other events, 557.8 us)
Sparse Core Ops, SparseCore 0:
  11.9 40.5 reduce-scatter.7
  269.7 40.5 reduce-scatter.9
  556.5 40.0 reduce-scatter.11
  861.2 40.0 reduce-scatter.13
  1167.5 87.8 all-reduce.6
